TPU v7x, 32 devices: a whole 2x2x4 slice. The times are simulated.
32 devices in a mesh: grp: 2 (over y), ka: 4 (over z), ga: 2 (over x), ba: 2 (over core).
Axes of the slice: x: 2, y: 2, z: 4, core: 2. Of those that a mesh axis runs over, the one named last changes fastest.
Arguments:
- coefficients: bfloat16 [2, 2, 16, 512, 9216], P(None, None, ('grp', 'ka'), 'ba', 'ga'), parts along dimension 2, may hold values from -1 to 1
- occupied: int32 [2, 16], P(None, ('grp', 'ka')), parts along dimension 1, may hold values from 64 to 512
- kweights: float32 [16], P(('grp', 'ka')), parts along dimension 0, may hold values from 0.5 to 2
- owner_map: int32 [1024], P('grp'), parts along dimension 0, may hold values from 0 to 7, as said below
- species: int32 [1024], P('grp'), parts along dimension 0, may hold values from 0 to 1
- positions: float32 [3, 1024], P(None, 'grp'), parts along dimension 1, may hold values from 0 to 100
- multipole: float32 [2, 9, 324], replicated, may hold values from -0.3125 to 0.3125
- widths: float32 [2], replicated, may hold values from 0.05 to 0.3
- potential: float32 [2, 442368], P(None, ('grp', 'ga')), parts along dimension 1, may hold values from -0.013671875 to 0.013671875
Outputs:
- density: float32 [2, 2, 1024, 324], P(None, None, ('grp', 'ka', 'ga', 'ba')), parts along dimension 2
- forces: float32 [3, 1024], P(None, ('grp', 'ka', 'ga', 'ba')), parts along dimension 1
There are 2 independent parts, one for each index of `grp`. A program takes and returns all parts, laid end to end along the dimension named above; an argument that names none is the same for every part. Nothing has to cross between parts.
Inputs may be any that keep to these rules, and one draw needn't show every extreme that they name: `owner_map`: within each aligned block of 256 atoms every owner number is named by exactly 32 atoms.
All inputs are finite; a program needn't handle non-finite values.
Results may differ from a plain program's by a relative error of at most 0.0003.
Values sent between devices are 32-bit elements; how exact they have to be, the bound alone decides.
A program may use at most 192 MiB of HBM per device.

v0:
```python
import jax
import jax.numpy as jnp
from jax import lax
from jax.sharding import PartitionSpec as P

NPROJ = 18
SPECIES = 2
NL = 9
GRID = 96
grid_step = 0.0625
highest = lax.Precision.HIGHEST


def harmonics(start_index, length, widths):
    indices = start_index + jnp.arange(length, dtype=jnp.int32)
    planes = [indices % GRID, indices // GRID % GRID, indices // (GRID * GRID)]
    vectors = []
    for plane_index in planes:
        signed = jnp.where(plane_index >= GRID // 2, plane_index - GRID, plane_index)
        vectors.append(grid_step * signed.astype(jnp.float32))
    along_x, along_y, along_z = vectors
    square = along_x * along_x + along_y * along_y + along_z * along_z
    shapes = jnp.stack(
        [
            jnp.ones_like(square),
            along_x,
            along_y,
            along_z,
            along_x * along_y,
            along_y * along_z,
            along_z * along_x,
            along_x * along_x - along_y * along_y,
            3.0 * along_z * along_z - square,
        ]
    )
    damping = jnp.exp(-widths[:, None] * square[None, :])
    form_table = (damping[:, None, :] * shapes[None, :, :]).reshape(SPECIES * NL, length)
    return (form_table, jnp.stack(vectors, axis=1))


def force_block(moments, places, form_table, vectors, pot_piece):
    smooth = jnp.dot(moments, form_table, precision=highest)
    phases = jnp.dot(places, vectors.T, precision=highest)
    wave_term = pot_piece[0][None, :] * jnp.sin(phases) + pot_piece[1][None, :] * jnp.cos(phases)
    return jnp.dot(smooth * wave_term, vectors, precision=highest)


def local_force(moments, places, pot_piece, start_index, widths):
    length = pot_piece.shape[1]
    pieces = 8
    width_block = length // pieces

    def gblock(running, number):
        offset = number * width_block
        form_table, vectors = harmonics(start_index + offset, width_block, widths)
        segment = lax.dynamic_slice_in_dim(pot_piece, offset, width_block, 1)
        return (running + force_block(moments, places, form_table, vectors, segment), None)

    result, unused = lax.scan(
        gblock, jnp.zeros((moments.shape[0], 3), jnp.float32), jnp.arange(pieces, dtype=jnp.int32)
    )
    return result


def shards(
    coefficients, occupied, kweights, owner_map, species, positions, multipole, widths, potential
):
    spin_count, complex_parts, kcount, bcount, columns = coefficients.shape
    atoms_blk = columns // NPROJ
    kgroups = lax.axis_size("ka")
    bgroups = lax.axis_size("ba")
    owners = kgroups * bgroups
    per_owner = atoms_blk // owners
    owner_index = lax.axis_index(("ka", "ba"))
    group_index = lax.axis_index("ga")
    band_index = lax.axis_index("ba") * bcount + jnp.arange(bcount, dtype=jnp.int32)
    band_mask = (band_index[None, None, :] < occupied[:, :, None]).astype(jnp.bfloat16)
    values = coefficients.reshape(spin_count, complex_parts, kcount, bcount, atoms_blk, NPROJ)
    masked = values * band_mask[:, None, :, :, None, None]
    real_part = jnp.einsum(
        "sckbai,sckbaj->skaij", values, masked, preferred_element_type=jnp.float32
    )
    cross_term = jnp.einsum(
        "skbai,skbaj->skaij", values[:, 0], masked[:, 1], preferred_element_type=jnp.float32
    )
    imag_part = cross_term - jnp.swapaxes(cross_term, 3, 4)
    weighted = jnp.stack([real_part, imag_part], axis=1) * kweights[None, None, :, None, None, None]
    density_local = jnp.sum(weighted, axis=2).reshape(
        spin_count, complex_parts, atoms_blk, NPROJ * NPROJ
    )
    ranking = jnp.argsort(owner_map.reshape(-1, atoms_blk), axis=1, stable=True)
    own_ranks = lax.dynamic_slice_in_dim(ranking, owner_index * per_owner, per_owner, 1)
    summed = lax.psum(density_local, ("ka", "ba"))
    own_rows = lax.dynamic_index_in_dim(own_ranks, group_index, 0, keepdims=False)
    own_density = jnp.take(summed, own_rows, axis=2)
    block_count = own_ranks.shape[0]
    atom_ids = jnp.arange(block_count, dtype=jnp.int32)[:, None] * atoms_blk + own_ranks
    own_atoms = lax.dynamic_index_in_dim(atom_ids, group_index, 0, keepdims=False)
    real_total = jnp.sum(own_density[:, 0], axis=0)
    selector = (
        jnp.take(species, own_atoms)[:, None] == jnp.arange(SPECIES, dtype=jnp.int32)[None, :]
    ).astype(jnp.float32)
    moments = jnp.dot(
        real_total, multipole.reshape(SPECIES * NL, NPROJ * NPROJ).T, precision=highest
    ) * jnp.repeat(selector, NL, axis=1)
    gcount = potential.shape[1]
    all_moments = lax.all_gather(moments, "ga", axis=0, tiled=True)
    places = jnp.take(positions, atom_ids.reshape(-1), axis=1).T
    partial_force = local_force(all_moments, places, potential, group_index * gcount, widths)
    summed_force = lax.psum(partial_force, "ga")
    own_force = lax.dynamic_slice_in_dim(summed_force, group_index * per_owner, per_owner, 0)
    return (own_density, own_force.T)


def solution(mesh):
    placed = (
        P(None, None, ("grp", "ka"), "ba", "ga"),
        P(None, ("grp", "ka")),
        P(("grp", "ka")),
        P("grp"),
        P("grp"),
        P(None, "grp"),
        P(),
        P(),
        P(None, ("grp", "ga")),
    )
    return jax.shard_map(
        shards,
        mesh=mesh,
        in_specs=placed,
        out_specs=(
            P(None, None, ("grp", "ka", "ga", "ba"), None),
            P(None, ("grp", "ka", "ga", "ba")),
        ),
        check_vma=False,
    )
```

profile of v0, /device:TPU:0, one launch (start us, length us, event | category | flops | bytes accessed | tf_op | source)
XLA Modules:
  0.0 663.2 jit_solution(12733213700706561287)
XLA Ops:
  10.0 45.7 %copy.45 = bf16[2,2,2,256,4608]{3,2,4,1,0:T(2,128)(2,1)} copy(bf16[2,2,2,256,4608]{4,3,2,1,0:T(8,128)(2,1)} %param.11) | data formatting | bytes 37748736 | tf_op args[0]
  55.7 45.4 %copy.46 = bf16[2,2,2,256,256,18]{4,3,5,2,1,0:T(8,128)(2,1)} copy(bf16[2,2,2,256,256,18]{3,2,5,4,1,0:T(2,128)(2,1)} %bitcast.68) | data formatting | bytes 37748736 | tf_op jit(solution)/shard_map/reshape | solution.py:78
  101.1 9.1 %slice.35 = bf16[2,1,2,256,256,18]{3,2,5,4,1,0:T(2,128)(2,1)} slice(bf16[2,2,2,256,256,18]{3,2,5,4,1,0:T(2,128)(2,1)} %bitcast.69), slice={[0:2], [0:1], [0:2], [0:256], [0:256], [0:18]} | slice | bytes 18874368 | tf_op jit(solution)/shard_map/slice | solution.py:84
  110.3 16.7 %broadcast_multiply_fusion.2 = bf16[2,2,2,256,256,18]{4,3,5,2,1,0:T(8,128)(2,1)} fusion(bf16[2,2,2,256,256,18]{4,3,5,2,1,0:T(8,128)(2,1)} %copy.46, bf16[2,2,256]{2,1,0:T(2,128)(2,1)S(1)} %compare_convert_fusion), kind=kLoop, calls=%fused_computation.84 | loop fusion | flops 9437184 | bytes 37750784 | tf_op jit(solution)/shard_map/mul | solution.py:79
  127.0 8.4 %slice_bitcast_fusion = bf16[2,2,256,256,18]{3,2,4,1,0:T(8,128)(2,1)} fusion(bf16[2,2,2,256,256,18]{4,3,5,2,1,0:T(8,128)(2,1)} %broadcast_multiply_fusion.2), kind=kLoop, calls=%fused_computation.83 | loop fusion | bytes 18874368 | tf_op jit(solution)/shard_map/squeeze | solution.py:84
  135.4 29.6 %copy.62 = bf16[2,2,2,256,256,18]{3,5,1,2,0,4:T(8,128)(2,1)} copy(bf16[2,2,2,256,256,18]{4,3,5,2,1,0:T(8,128)(2,1)} %broadcast_multiply_fusion.2) | data formatting | bytes 37748736 | tf_op jit(solution)/shard_map/mul | solution.py:79
  165.1 15.5 %copy.50 = bf16[2,2,256,256,18]{2,4,3,1,0:T(8,128)(2,1)} copy(bf16[2,2,256,256,18]{3,2,4,1,0:T(8,128)(2,1)} %slice_bitcast_fusion) | data formatting | bytes 18874368 | tf_op jit(solution)/shard_map/squeeze | solution.py:84
  180.6 13.3 %fusion.40 = f32[2,2,256,18,18]{4,3,2,1,0:T(8,128)} fusion(bf16[2,2,256,256,18]{2,4,3,1,0:T(8,128)(2,1)} %copy.50, bf16[2,1,2,256,256,18]{3,2,5,4,1,0:T(2,128)(2,1)} %slice.35), kind=kOutput, calls=%fused_computation.80 | convolution fusion | flops 169869312 | bytes 20201472 | tf_op jit(solution)/shard_map/skbai,skbaj->skaij/dot_general | solution.py:83
  193.9 14.0 %copy.51 = f32[2,2,256,18,18]{3,4,2,1,0:T(8,128)} copy(f32[2,2,256,18,18]{4,3,2,1,0:T(8,128)} %fusion.40) | data formatting | bytes 2654208 | tf_op jit(solution)/shard_map/skbai,skbaj->skaij/dot_general | solution.py:83
  207.9 14.1 %fusion.41 = f32[2,1,2,256,18,18]{5,4,3,2,0,1:T(8,128)} fusion(f32[2,2,256,18,18]{4,3,2,1,0:T(8,128)} %fusion.40, f32[2,2,256,18,18]{3,4,2,1,0:T(8,128)} %copy.51), kind=kLoop, calls=%fused_computation.82 | loop fusion | flops 331776 | bytes 3981312 | tf_op jit(solution)/shard_map/stack | solution.py:87
  221.9 11.4 %copy.53 = f32[2,1,2,256,18,18]{3,2,5,4,1,0:T(2,128)S(1)} copy(f32[2,1,2,256,18,18]{5,4,3,2,0,1:T(8,128)} %fusion.41) | data formatting | bytes 2654208 | tf_op jit(solution)/shard_map/stack | solution.py:87
  233.4 21.8 %fusion.42 = f32[2,1,2,256,18,18]{4,5,2,0,3,1:T(8,128)} fusion(bf16[2,2,2,256,256,18]{3,5,1,2,0,4:T(8,128)(2,1)} %copy.62, bf16[2,2,2,256,256,18]{3,2,5,4,1,0:T(2,128)(2,1)} %bitcast.70), kind=kOutput, calls=%fused_computation.85 | convolution fusion | flops 339738624 | bytes 39075840 | tf_op jit(solution)/shard_map/sckbai,sckbaj->skaij/dot_general | solution.py:80
  255.1 11.6 %copy.52 = f32[2,1,2,256,18,18]{3,2,5,4,1,0:T(2,128)S(1)} copy(f32[2,1,2,256,18,18]{4,5,2,0,3,1:T(8,128)} %fusion.42) | data formatting | bytes 2654208 | tf_op jit(solution)/shard_map/stack | solution.py:87
  266.8 3.7 fusion.45
  271.6 2.4 copy.56
  278.9 60.1 %all-reduce.2.cloned.1.call-done = f32[2,2,256,324]{3,1,2,0:T(2,128)} async-done(((f32[2,2,256,324]{3,1,2,0:T(2,128)}), f32[2,2,256,324]{3,1,2,0:T(2,128)}) %all-reduce.2.cloned.1.call-update) | async-done | bytes 1327120 | tf_op jit(solution)/shard_map/psum | solution.py:93
  339.0 2.2 gather_fusion
  342.3 4.4 all-gather
  346.8 303.3 %while.14 = (s32[]{:T(128)}, f32[64,3]{0,1:T(4,128)}, f32[2,1]{0,1:T(1,128)S(1)}, s32[8]{0:T(128)S(1)}, s32[]{:T(128)}, /*index=5*/f32[64,18]{0,1:T(8,128)S(1)},...) while((s32[]{:T(128)}, f32[64,3]{0,1:T(4,128)}, ...), condition=%wide.region_5.6_spmd.clone, body=%wide.region_4.5_spmd.clone.sunk | while | flops 262103424 | bytes 21960220 | solution.py:59
  356.1 3.7 fusion.77
  359.8 1.3 dynamic-slice_reduce_fusion.3
  361.2 18.2 %convolution_multiply_fusion.3 = f32[13824,64]{0,1:T(8,128)} fusion(f32[18,13824]{1,0:T(8,128)} %mul.712, f32[64,18]{0,1:T(8,128)S(1)} %get-tuple-element.353, f32[13824,64]{0,1:T(8,128)S(1)} %fusion.77, f32[13824]{0:T(1024)S(1)} %get-tuple-element.318, f32[13824]{0:T(1024)S(1)} %get-tuple-element.319), kind=kOutput, calls=%fused_computation.3.clone.1 | convolution fusion | flops 194641920 | bytes 8188416 | tf_op jit(solution)/shard_map/while/body/eval_jaxpr/dot_general | solution.py:42
  379.4 5.5 convolution_add_fusion.2
  394.0 3.7 fusion.77
  397.7 1.3 dynamic-slice_reduce_fusion.3
  399.1 18.2 %convolution_multiply_fusion.3 = f32[13824,64]{0,1:T(8,128)} fusion(f32[18,13824]{1,0:T(8,128)} %mul.712, f32[64,18]{0,1:T(8,128)S(1)} %get-tuple-element.353, f32[13824,64]{0,1:T(8,128)S(1)} %fusion.77, f32[13824]{0:T(1024)S(1)} %get-tuple-element.318, f32[13824]{0:T(1024)S(1)} %get-tuple-element.319), kind=kOutput, calls=%fused_computation.3.clone.1 | convolution fusion | flops 194641920 | bytes 8188416 | tf_op jit(solution)/shard_map/while/body/eval_jaxpr/dot_general | solution.py:42
  417.3 5.5 convolution_add_fusion.2
  431.9 3.7 fusion.77
  435.6 1.3 dynamic-slice_reduce_fusion.3
  436.9 18.2 %convolution_multiply_fusion.3 = f32[13824,64]{0,1:T(8,128)} fusion(f32[18,13824]{1,0:T(8,128)} %mul.712, f32[64,18]{0,1:T(8,128)S(1)} %get-tuple-element.353, f32[13824,64]{0,1:T(8,128)S(1)} %fusion.77, f32[13824]{0:T(1024)S(1)} %get-tuple-element.318, f32[13824]{0:T(1024)S(1)} %get-tuple-element.319), kind=kOutput, calls=%fused_computation.3.clone.1 | convolution fusion | flops 194641920 | bytes 8188416 | tf_op jit(solution)/shard_map/while/body/eval_jaxpr/dot_general | solution.py:42
  455.2 5.5 convolution_add_fusion.2
  469.8 3.7 fusion.77
  474.8 18.2 %convolution_multiply_fusion.3 = f32[13824,64]{0,1:T(8,128)} fusion(f32[18,13824]{1,0:T(8,128)} %mul.712, f32[64,18]{0,1:T(8,128)S(1)} %get-tuple-element.353, f32[13824,64]{0,1:T(8,128)S(1)} %fusion.77, f32[13824]{0:T(1024)S(1)} %get-tuple-element.318, f32[13824]{0:T(1024)S(1)} %get-tuple-element.319), kind=kOutput, calls=%fused_computation.3.clone.1 | convolution fusion | flops 194641920 | bytes 8188416 | tf_op jit(solution)/shard_map/while/body/eval_jaxpr/dot_general | solution.py:42
  493.0 5.5 convolution_add_fusion.2
  507.7 3.7 fusion.77
  512.7 18.2 %convolution_multiply_fusion.3 = f32[13824,64]{0,1:T(8,128)} fusion(f32[18,13824]{1,0:T(8,128)} %mul.712, f32[64,18]{0,1:T(8,128)S(1)} %get-tuple-element.353, f32[13824,64]{0,1:T(8,128)S(1)} %fusion.77, f32[13824]{0:T(1024)S(1)} %get-tuple-element.318, f32[13824]{0:T(1024)S(1)} %get-tuple-element.319), kind=kOutput, calls=%fused_computation.3.clone.1 | convolution fusion | flops 194641920 | bytes 8188416 | tf_op jit(solution)/shard_map/while/body/eval_jaxpr/dot_general | solution.py:42
  530.9 5.5 convolution_add_fusion.2
  545.6 3.7 fusion.77
  550.6 18.2 %convolution_multiply_fusion.3 = f32[13824,64]{0,1:T(8,128)} fusion(f32[18,13824]{1,0:T(8,128)} %mul.712, f32[64,18]{0,1:T(8,128)S(1)} %get-tuple-element.353, f32[13824,64]{0,1:T(8,128)S(1)} %fusion.77, f32[13824]{0:T(1024)S(1)} %get-tuple-element.318, f32[13824]{0:T(1024)S(1)} %get-tuple-element.319), kind=kOutput, calls=%fused_computation.3.clone.1 | convolution fusion | flops 194641920 | bytes 8188416 | tf_op jit(solution)/shard_map/while/body/eval_jaxpr/dot_general | solution.py:42
  568.8 5.5 convolution_add_fusion.2
  583.5 3.7 fusion.77
  588.5 18.2 %convolution_multiply_fusion.3 = f32[13824,64]{0,1:T(8,128)} fusion(f32[18,13824]{1,0:T(8,128)} %mul.712, f32[64,18]{0,1:T(8,128)S(1)} %get-tuple-element.353, f32[13824,64]{0,1:T(8,128)S(1)} %fusion.77, f32[13824]{0:T(1024)S(1)} %get-tuple-element.318, f32[13824]{0:T(1024)S(1)} %get-tuple-element.319), kind=kOutput, calls=%fused_computation.3.clone.1 | convolution fusion | flops 194641920 | bytes 8188416 | tf_op jit(solution)/shard_map/while/body/eval_jaxpr/dot_general | solution.py:42
  606.7 5.5 convolution_add_fusion.2
  621.4 3.7 fusion.77
  625.1 1.3 dynamic-slice_reduce_fusion.3
  626.4 18.2 %convolution_multiply_fusion.3 = f32[13824,64]{0,1:T(8,128)} fusion(f32[18,13824]{1,0:T(8,128)} %mul.712, f32[64,18]{0,1:T(8,128)S(1)} %get-tuple-element.353, f32[13824,64]{0,1:T(8,128)S(1)} %fusion.77, f32[13824]{0:T(1024)S(1)} %get-tuple-element.318, f32[13824]{0:T(1024)S(1)} %get-tuple-element.319), kind=kOutput, calls=%fused_computation.3.clone.1 | convolution fusion | flops 194641920 | bytes 8188416 | tf_op jit(solution)/shard_map/while/body/eval_jaxpr/dot_general | solution.py:42
  644.6 5.5 convolution_add_fusion.2
  650.2 4.9 psum.15
  (275 shorter events, 82.4 us)
Async XLA Ops:
  8.0 267.3 %copy-start = (s32[512]{0:T(512)S(1)}, s32[512]{0:T(512)}, u32[]{:S(2)}) copy-start(s32[512]{0:T(512)} %param.15) | copy-start | bytes 6148
  8.0 266.3 %sort.19.cloned.1.call-start = ((), (), s32[]{:S(2)}) async-start(), calls=%async_computation.1 | async-start | bytes 12320 | tf_op jit(solution)/shard_map/jit(argsort)/sort | solution.py:91
  9.9 329.0 %all-reduce.2.cloned.1.call-start = ((), (), s32[]{:S(2)}) async-start(), calls=%async_computation | async-start | bytes 3145728 | tf_op jit(solution)/shard_map/psum | solution.py:93
  101.1 9.1 %copy-start.8 = (s32[2,2]{1,0:T(2,128)S(1)}, s32[2,2]{1,0:T(2,128)}, u32[]{:S(2)}) copy-start(s32[2,2]{1,0:T(2,128)} %param.12) | copy-start | bytes 52
  255.1 11.6 %copy-start.9 = (f32[2]{0:T(128)S(1)}, f32[2]{0:T(128)}, u32[]{:S(2)}) copy-start(f32[2]{0:T(128)} %param.13) | copy-start | bytes 28
  270.5 3.6 copy-start.10
  270.5 3.6 copy-start.4
  270.6 3.6 copy-start.7
  347.0 6.4 copy-start.5
  356.1 3.7 copy-start.2
  356.1 3.7 copy-start.3
  379.4 5.5 copy-start.6
  379.4 5.5 copy-start.12
  384.9 6.4 copy-start.5
  394.0 3.7 copy-start.2
  394.0 3.7 copy-start.3
  417.3 5.5 copy-start.6
  417.3 5.5 copy-start.12
  422.8 6.4 copy-start.5
  431.9 3.7 copy-start.2
  431.9 3.7 copy-start.3
  455.2 5.5 copy-start.6
  455.2 5.5 copy-start.12
  460.7 6.4 copy-start.5
  469.8 3.7 copy-start.2
  469.8 3.7 copy-start.3
  493.0 5.5 copy-start.6
  493.0 5.5 copy-start.12
  498.6 6.4 copy-start.5
  507.7 3.7 copy-start.2
  507.7 3.7 copy-start.3
  530.9 5.5 copy-start.6
  530.9 5.5 copy-start.12
  536.5 6.4 copy-start.5
  545.6 3.7 copy-start.2
  545.6 3.7 copy-start.3
  568.8 5.5 copy-start.6
  568.8 5.5 copy-start.12
  574.4 6.4 copy-start.5
  583.5 3.7 copy-start.2
  583.5 3.7 copy-start.3
  606.7 5.5 copy-start.6
  606.7 5.5 copy-start.12
  612.3 6.4 copy-start.5
  621.3 3.7 copy-start.2
  621.4 3.7 copy-start.3
  644.6 5.5 copy-start.6
  644.6 5.5 copy-start.12
  (16 other events, 16.1 us)
Sparse Core Ops, SparseCore 0:
  11.7 2.2 sort.21.cloned.1.call-done
  (1 shorter events, 0.0 us)
Sparse Core Ops, SparseCore 1:
  274.1 64.8 all-reduce.1
where the time goes:
time: 668 us; the launch traced here: 663 us
  matrix products  255 us (38%)
  local copies, waits for them, and re-layouts  234 us (35%)
  other arithmetic  83.3 us (12%)
  waiting for transfers between devices  60.1 us (9%)
  between operations  15.7 us (2%)
  blocking collectives  9.31 us (1%)
    dot_general x8, matrix products, force_block(): smooth = jnp.dot(moments, form_table, precision=highest)  146 us
    psum x1, waiting for transfers between devices, shards(): summed = lax.psum(density_local, ('ka', 'ba'))  60.1 us
    unnamed x19, local copies, waits for them, and re-layouts  47.3 us
    reshape x1, local copies, waits for them, and re-layouts, shards(): coefficients.reshape(spin_count, complex_parts, kcount, bcount, atoms_blk...  45.4 us
    dot_general x8, matrix products, force_block(): return jnp.dot(smooth * wave_term, vectors, precision=highest)  44.3 us
    mul x1, local copies, waits for them, and re-layouts, shards(): masked = values * band_mask[:, None, :, :, None, None]  29.6 us
    dot_general x8, matrix products, force_block(): phases = jnp.dot(places, vectors.T, precision=highest)  29.6 us
    squeeze x2, local copies, waits for them, and re-layouts, shards(): masked[:, 1]  23.9 us
  transfers between devices with their start and end apart: 1, of which 1 were waited for; matrix products, arithmetic and copies ran while one was open for 1% of the time, Pallas kernels for 0%

commit v1 on v0

--- a/solution.py
+++ b/solution.py
@@ -90,7 +90,7 @@
     )
     ranking = jnp.argsort(owner_map.reshape(-1, atoms_blk), axis=1, stable=True)
     own_ranks = lax.dynamic_slice_in_dim(ranking, owner_index * per_owner, per_owner, 1)
-    summed = lax.psum(density_local, ("ka", "ba"))
+    summed = lax.psum(lax.psum(density_local, axis_name="ba"), axis_name="ka")
     own_rows = lax.dynamic_index_in_dim(own_ranks, group_index, 0, keepdims=False)
     own_density = jnp.take(summed, own_rows, axis=2)
     block_count = own_ranks.shape[0]

time: 668 us -> 698 us (1.045)
  waiting for transfers between devices: 60.1 us -> 90.1 us
    psum x1 -> x2, waiting for transfers between devices: 60.1 us -> 90.1 us  [shards(): summed = lax.psum(lax.psum(density_local, axis_name='ba'), axis_name='ka')]
  transfers between devices with their start and end apart: 1 -> 2, of which waited for: 1 -> 2; matrix products, arithmetic and copies ran while one was open for 1% -> 1% of each run, Pallas kernels for 0% -> 0%
where the time goes in v1:
time: 698 us; the launch traced here: 693 us
  matrix products  255 us (37%)
  local copies, waits for them, and re-layouts  234 us (34%)
  waiting for transfers between devices  90.1 us (13%)
  other arithmetic  83.3 us (12%)
  between operations  15.8 us (2%)
  blocking collectives  9.31 us (1%)
    dot_general x8, matrix products, force_block(): smooth = jnp.dot(moments, form_table, precision=highest)  146 us
    psum x2, waiting for transfers between devices, shards(): summed = lax.psum(lax.psum(density_local, axis_name='ba'), axis_name='ka')  90.1 us
    unnamed x19, local copies, waits for them, and re-layouts  47.3 us
    reshape x1, local copies, waits for them, and re-layouts, shards(): coefficients.reshape(spin_count, complex_parts, kcount, bcount, atoms_blk...  45.4 us
    dot_general x8, matrix products, force_block(): return jnp.dot(smooth * wave_term, vectors, precision=highest)  44.3 us
    mul x1, local copies, waits for them, and re-layouts, shards(): masked = values * band_mask[:, None, :, :, None, None]  29.6 us
    dot_general x8, matrix products, force_block(): phases = jnp.dot(places, vectors.T, precision=highest)  29.6 us
    squeeze x2, local copies, waits for them, and re-layouts, shards(): masked[:, 1]  23.9 us
  transfers between devices with their start and end apart: 2, of which 2 were waited for; matrix products, arithmetic and copies ran while one was open for 1% of the time, Pallas kernels for 0%

profile of v1, /device:TPU:0, one launch (start us, length us, event | category | flops | bytes accessed | tf_op | source)
XLA Modules:
  0.0 693.1 jit_solution(1047650428505457892)
XLA Ops:
  10.0 45.7 %copy.45 = bf16[2,2,2,256,4608]{3,2,4,1,0:T(2,128)(2,1)} copy(bf16[2,2,2,256,4608]{4,3,2,1,0:T(8,128)(2,1)} %param.11) | data formatting | bytes 37748736 | tf_op args[0]
  55.7 45.4 %copy.46 = bf16[2,2,2,256,256,18]{4,3,5,2,1,0:T(8,128)(2,1)} copy(bf16[2,2,2,256,256,18]{3,2,5,4,1,0:T(2,128)(2,1)} %bitcast.68) | data formatting | bytes 37748736 | tf_op jit(solution)/shard_map/reshape | solution.py:78
  101.1 9.1 %slice.35 = bf16[2,1,2,256,256,18]{3,2,5,4,1,0:T(2,128)(2,1)} slice(bf16[2,2,2,256,256,18]{3,2,5,4,1,0:T(2,128)(2,1)} %bitcast.69), slice={[0:2], [0:1], [0:2], [0:256], [0:256], [0:18]} | slice | bytes 18874368 | tf_op jit(solution)/shard_map/slice | solution.py:84
  110.3 16.7 %broadcast_multiply_fusion.2 = bf16[2,2,2,256,256,18]{4,3,5,2,1,0:T(8,128)(2,1)} fusion(bf16[2,2,2,256,256,18]{4,3,5,2,1,0:T(8,128)(2,1)} %copy.46, bf16[2,2,256]{2,1,0:T(2,128)(2,1)S(1)} %compare_convert_fusion), kind=kLoop, calls=%fused_computation.84 | loop fusion | flops 9437184 | bytes 37750784 | tf_op jit(solution)/shard_map/mul | solution.py:79
  127.0 8.4 %slice_bitcast_fusion = bf16[2,2,256,256,18]{3,2,4,1,0:T(8,128)(2,1)} fusion(bf16[2,2,2,256,256,18]{4,3,5,2,1,0:T(8,128)(2,1)} %broadcast_multiply_fusion.2), kind=kLoop, calls=%fused_computation.83 | loop fusion | bytes 18874368 | tf_op jit(solution)/shard_map/squeeze | solution.py:84
  135.4 29.6 %copy.62 = bf16[2,2,2,256,256,18]{3,5,1,2,0,4:T(8,128)(2,1)} copy(bf16[2,2,2,256,256,18]{4,3,5,2,1,0:T(8,128)(2,1)} %broadcast_multiply_fusion.2) | data formatting | bytes 37748736 | tf_op jit(solution)/shard_map/mul | solution.py:79
  165.1 15.5 %copy.50 = bf16[2,2,256,256,18]{2,4,3,1,0:T(8,128)(2,1)} copy(bf16[2,2,256,256,18]{3,2,4,1,0:T(8,128)(2,1)} %slice_bitcast_fusion) | data formatting | bytes 18874368 | tf_op jit(solution)/shard_map/squeeze | solution.py:84
  180.6 13.3 %fusion.40 = f32[2,2,256,18,18]{4,3,2,1,0:T(8,128)} fusion(bf16[2,2,256,256,18]{2,4,3,1,0:T(8,128)(2,1)} %copy.50, bf16[2,1,2,256,256,18]{3,2,5,4,1,0:T(2,128)(2,1)} %slice.35), kind=kOutput, calls=%fused_computation.80 | convolution fusion | flops 169869312 | bytes 20201472 | tf_op jit(solution)/shard_map/skbai,skbaj->skaij/dot_general | solution.py:83
  193.9 14.0 %copy.51 = f32[2,2,256,18,18]{3,4,2,1,0:T(8,128)} copy(f32[2,2,256,18,18]{4,3,2,1,0:T(8,128)} %fusion.40) | data formatting | bytes 2654208 | tf_op jit(solution)/shard_map/skbai,skbaj->skaij/dot_general | solution.py:83
  207.9 14.1 %fusion.41 = f32[2,1,2,256,18,18]{5,4,3,2,0,1:T(8,128)} fusion(f32[2,2,256,18,18]{4,3,2,1,0:T(8,128)} %fusion.40, f32[2,2,256,18,18]{3,4,2,1,0:T(8,128)} %copy.51), kind=kLoop, calls=%fused_computation.82 | loop fusion | flops 331776 | bytes 3981312 | tf_op jit(solution)/shard_map/stack | solution.py:87
  221.9 11.4 %copy.53 = f32[2,1,2,256,18,18]{3,2,5,4,1,0:T(2,128)S(1)} copy(f32[2,1,2,256,18,18]{5,4,3,2,0,1:T(8,128)} %fusion.41) | data formatting | bytes 2654208 | tf_op jit(solution)/shard_map/stack | solution.py:87
  233.4 21.8 %fusion.42 = f32[2,1,2,256,18,18]{4,5,2,0,3,1:T(8,128)} fusion(bf16[2,2,2,256,256,18]{3,5,1,2,0,4:T(8,128)(2,1)} %copy.62, bf16[2,2,2,256,256,18]{3,2,5,4,1,0:T(2,128)(2,1)} %bitcast.70), kind=kOutput, calls=%fused_computation.85 | convolution fusion | flops 339738624 | bytes 39075840 | tf_op jit(solution)/shard_map/sckbai,sckbaj->skaij/dot_general | solution.py:80
  255.1 11.6 %copy.52 = f32[2,1,2,256,18,18]{3,2,5,4,1,0:T(2,128)S(1)} copy(f32[2,1,2,256,18,18]{4,5,2,0,3,1:T(8,128)} %fusion.42) | data formatting | bytes 2654208 | tf_op jit(solution)/shard_map/stack | solution.py:87
  266.8 3.7 fusion.45
  271.6 2.4 copy.56
  276.1 20.8 %all-reduce.3.cloned.1.call-done = f32[2,2,256,324]{3,1,2,0:T(2,128)} async-done(((f32[2,2,256,324]{3,1,2,0:T(2,128)}), f32[2,2,256,324]{3,1,2,0:T(2,128)}) %all-reduce.3.cloned.1.call-update) | async-done | bytes 1327120 | tf_op jit(solution)/shard_map/psum | solution.py:93
  299.8 69.3 %all-reduce.5.cloned.1.call-done = f32[2,2,256,324]{3,1,2,0:T(2,128)} async-done(((f32[2,2,256,324]{3,1,2,0:T(2,128)}), f32[2,2,256,324]{3,1,2,0:T(2,128)}) %all-reduce.5.cloned.1.call-update) | async-done | bytes 1327120 | tf_op jit(solution)/shard_map/psum | solution.py:93
  369.1 2.2 gather_fusion
  372.4 4.4 all-gather
  376.9 303.2 %while.14 = (s32[]{:T(128)}, f32[64,3]{0,1:T(4,128)}, f32[2,1]{0,1:T(1,128)S(1)}, s32[8]{0:T(128)S(1)}, s32[]{:T(128)}, /*index=5*/f32[64,18]{0,1:T(8,128)S(1)},...) while((s32[]{:T(128)}, f32[64,3]{0,1:T(4,128)}, ...), condition=%wide.region_6.7_spmd.clone, body=%wide.region_5.6_spmd.clone.sunk | while | flops 262103424 | bytes 21960220 | solution.py:59
  386.2 3.7 fusion.77
  389.9 1.3 dynamic-slice_reduce_fusion.3
  391.2 18.2 %convolution_multiply_fusion.3 = f32[13824,64]{0,1:T(8,128)} fusion(f32[18,13824]{1,0:T(8,128)} %mul.712, f32[64,18]{0,1:T(8,128)S(1)} %get-tuple-element.353, f32[13824,64]{0,1:T(8,128)S(1)} %fusion.77, f32[13824]{0:T(1024)S(1)} %get-tuple-element.318, f32[13824]{0:T(1024)S(1)} %get-tuple-element.319), kind=kOutput, calls=%fused_computation.3.clone.1 | convolution fusion | flops 194641920 | bytes 8188416 | tf_op jit(solution)/shard_map/while/body/eval_jaxpr/dot_general | solution.py:42
  409.5 5.5 convolution_add_fusion.2
  424.1 3.7 fusion.77
  427.8 1.3 dynamic-slice_reduce_fusion.3
  429.1 18.2 %convolution_multiply_fusion.3 = f32[13824,64]{0,1:T(8,128)} fusion(f32[18,13824]{1,0:T(8,128)} %mul.712, f32[64,18]{0,1:T(8,128)S(1)} %get-tuple-element.353, f32[13824,64]{0,1:T(8,128)S(1)} %fusion.77, f32[13824]{0:T(1024)S(1)} %get-tuple-element.318, f32[13824]{0:T(1024)S(1)} %get-tuple-element.319), kind=kOutput, calls=%fused_computation.3.clone.1 | convolution fusion | flops 194641920 | bytes 8188416 | tf_op jit(solution)/shard_map/while/body/eval_jaxpr/dot_general | solution.py:42
  447.3 5.5 convolution_add_fusion.2
  462.0 3.7 fusion.77
  467.0 18.2 %convolution_multiply_fusion.3 = f32[13824,64]{0,1:T(8,128)} fusion(f32[18,13824]{1,0:T(8,128)} %mul.712, f32[64,18]{0,1:T(8,128)S(1)} %get-tuple-element.353, f32[13824,64]{0,1:T(8,128)S(1)} %fusion.77, f32[13824]{0:T(1024)S(1)} %get-tuple-element.318, f32[13824]{0:T(1024)S(1)} %get-tuple-element.319), kind=kOutput, calls=%fused_computation.3.clone.1 | convolution fusion | flops 194641920 | bytes 8188416 | tf_op jit(solution)/shard_map/while/body/eval_jaxpr/dot_general | solution.py:42
  485.2 5.5 convolution_add_fusion.2
  499.8 3.7 fusion.77
  504.9 18.2 %convolution_multiply_fusion.3 = f32[13824,64]{0,1:T(8,128)} fusion(f32[18,13824]{1,0:T(8,128)} %mul.712, f32[64,18]{0,1:T(8,128)S(1)} %get-tuple-element.353, f32[13824,64]{0,1:T(8,128)S(1)} %fusion.77, f32[13824]{0:T(1024)S(1)} %get-tuple-element.318, f32[13824]{0:T(1024)S(1)} %get-tuple-element.319), kind=kOutput, calls=%fused_computation.3.clone.1 | convolution fusion | flops 194641920 | bytes 8188416 | tf_op jit(solution)/shard_map/while/body/eval_jaxpr/dot_general | solution.py:42
  523.1 5.5 convolution_add_fusion.2
  537.7 3.7 fusion.77
  542.8 18.2 %convolution_multiply_fusion.3 = f32[13824,64]{0,1:T(8,128)} fusion(f32[18,13824]{1,0:T(8,128)} %mul.712, f32[64,18]{0,1:T(8,128)S(1)} %get-tuple-element.353, f32[13824,64]{0,1:T(8,128)S(1)} %fusion.77, f32[13824]{0:T(1024)S(1)} %get-tuple-element.318, f32[13824]{0:T(1024)S(1)} %get-tuple-element.319), kind=kOutput, calls=%fused_computation.3.clone.1 | convolution fusion | flops 194641920 | bytes 8188416 | tf_op jit(solution)/shard_map/while/body/eval_jaxpr/dot_general | solution.py:42
  561.0 5.5 convolution_add_fusion.2
  575.6 3.7 fusion.77
  579.3 1.3 dynamic-slice_reduce_fusion.3
  580.6 18.2 %convolution_multiply_fusion.3 = f32[13824,64]{0,1:T(8,128)} fusion(f32[18,13824]{1,0:T(8,128)} %mul.712, f32[64,18]{0,1:T(8,128)S(1)} %get-tuple-element.353, f32[13824,64]{0,1:T(8,128)S(1)} %fusion.77, f32[13824]{0:T(1024)S(1)} %get-tuple-element.318, f32[13824]{0:T(1024)S(1)} %get-tuple-element.319), kind=kOutput, calls=%fused_computation.3.clone.1 | convolution fusion | flops 194641920 | bytes 8188416 | tf_op jit(solution)/shard_map/while/body/eval_jaxpr/dot_general | solution.py:42
  598.8 5.5 convolution_add_fusion.2
  613.5 3.7 fusion.77
  618.5 18.2 %convolution_multiply_fusion.3 = f32[13824,64]{0,1:T(8,128)} fusion(f32[18,13824]{1,0:T(8,128)} %mul.712, f32[64,18]{0,1:T(8,128)S(1)} %get-tuple-element.353, f32[13824,64]{0,1:T(8,128)S(1)} %fusion.77, f32[13824]{0:T(1024)S(1)} %get-tuple-element.318, f32[13824]{0:T(1024)S(1)} %get-tuple-element.319), kind=kOutput, calls=%fused_computation.3.clone.1 | convolution fusion | flops 194641920 | bytes 8188416 | tf_op jit(solution)/shard_map/while/body/eval_jaxpr/dot_general | solution.py:42
  636.7 5.5 convolution_add_fusion.2
  651.4 3.7 fusion.77
  656.4 18.2 %convolution_multiply_fusion.3 = f32[13824,64]{0,1:T(8,128)} fusion(f32[18,13824]{1,0:T(8,128)} %mul.712, f32[64,18]{0,1:T(8,128)S(1)} %get-tuple-element.353, f32[13824,64]{0,1:T(8,128)S(1)} %fusion.77, f32[13824]{0:T(1024)S(1)} %get-tuple-element.318, f32[13824]{0:T(1024)S(1)} %get-tuple-element.319), kind=kOutput, calls=%fused_computation.3.clone.1 | convolution fusion | flops 194641920 | bytes 8188416 | tf_op jit(solution)/shard_map/while/body/eval_jaxpr/dot_general | solution.py:42
  674.6 5.5 convolution_add_fusion.2
  680.1 4.9 psum.23
  (278 shorter events, 83.8 us)
Async XLA Ops:
  8.0 267.3 %copy-start = (s32[512]{0:T(512)S(1)}, s32[512]{0:T(512)}, u32[]{:S(2)}) copy-start(s32[512]{0:T(512)} %param.15) | copy-start | bytes 6148
  8.0 266.4 %sort.19.cloned.1.call-start = ((), (), s32[]{:S(2)}) async-start(), calls=%async_computation.2 | async-start | bytes 12320 | tf_op jit(solution)/shard_map/jit(argsort)/sort | solution.py:91
  9.9 286.9 %all-reduce.3.cloned.1.call-start = ((), (), s32[]{:S(2)}) async-start(), calls=%async_computation | async-start | bytes 3145728 | tf_op jit(solution)/shard_map/psum | solution.py:93
  101.1 9.1 %copy-start.8 = (s32[2,2]{1,0:T(2,128)S(1)}, s32[2,2]{1,0:T(2,128)}, u32[]{:S(2)}) copy-start(s32[2,2]{1,0:T(2,128)} %param.12) | copy-start | bytes 52
  255.1 11.6 %copy-start.9 = (f32[2]{0:T(128)S(1)}, f32[2]{0:T(128)}, u32[]{:S(2)}) copy-start(f32[2]{0:T(128)} %param.13) | copy-start | bytes 28
  270.6 3.8 copy-start.10
  274.1 95.0 %all-reduce.5.cloned.1.call-start = ((), (), s32[]{:S(2)}) async-start(), calls=%async_computation.1 | async-start | bytes 3145728 | tf_op jit(solution)/shard_map/psum | solution.py:93
  377.1 7.8 %copy-start.5 = (f32[2,1]{0,1:T(1,128)}, f32[2,1]{0,1:T(1,128)S(1)}, u32[]{:S(2)}) copy-start(f32[2,1]{0,1:T(1,128)S(1)} %get-tuple-element.350) | copy-start | bytes 28 | tf_op jit(solution)/shard_map/while
  377.1 7.8 %copy-start.11 = (s32[8]{0:T(128)}, s32[8]{0:T(128)S(1)}, u32[]{:S(2)}) copy-start(s32[8]{0:T(128)S(1)} %get-tuple-element.351) | copy-start | bytes 100 | tf_op jit(solution)/shard_map/while
  386.2 3.7 copy-start.2
  386.2 3.7 copy-start.3
  409.4 5.5 copy-start.6
  409.5 5.5 copy-start.12
  415.0 7.8 %copy-start.5 = (f32[2,1]{0,1:T(1,128)}, f32[2,1]{0,1:T(1,128)S(1)}, u32[]{:S(2)}) copy-start(f32[2,1]{0,1:T(1,128)S(1)} %get-tuple-element.350) | copy-start | bytes 28 | tf_op jit(solution)/shard_map/while
  415.0 7.8 %copy-start.11 = (s32[8]{0:T(128)}, s32[8]{0:T(128)S(1)}, u32[]{:S(2)}) copy-start(s32[8]{0:T(128)S(1)} %get-tuple-element.351) | copy-start | bytes 100 | tf_op jit(solution)/shard_map/while
  447.3 5.5 copy-start.6
  447.3 5.5 copy-start.12
  452.9 7.8 %copy-start.5 = (f32[2,1]{0,1:T(1,128)}, f32[2,1]{0,1:T(1,128)S(1)}, u32[]{:S(2)}) copy-start(f32[2,1]{0,1:T(1,128)S(1)} %get-tuple-element.350) | copy-start | bytes 28 | tf_op jit(solution)/shard_map/while
  452.9 7.8 %copy-start.11 = (s32[8]{0:T(128)}, s32[8]{0:T(128)S(1)}, u32[]{:S(2)}) copy-start(s32[8]{0:T(128)S(1)} %get-tuple-element.351) | copy-start | bytes 100 | tf_op jit(solution)/shard_map/while
  461.9 3.7 copy-start.2
  461.9 3.7 copy-start.3
  485.2 5.5 copy-start.6
  485.2 5.5 copy-start.12
  490.8 7.8 %copy-start.5 = (f32[2,1]{0,1:T(1,128)}, f32[2,1]{0,1:T(1,128)S(1)}, u32[]{:S(2)}) copy-start(f32[2,1]{0,1:T(1,128)S(1)} %get-tuple-element.350) | copy-start | bytes 28 | tf_op jit(solution)/shard_map/while
  490.8 7.8 %copy-start.11 = (s32[8]{0:T(128)}, s32[8]{0:T(128)S(1)}, u32[]{:S(2)}) copy-start(s32[8]{0:T(128)S(1)} %get-tuple-element.351) | copy-start | bytes 100 | tf_op jit(solution)/shard_map/while
  499.8 3.7 copy-start.2
  499.8 3.7 copy-start.3
  523.1 5.5 copy-start.6
  523.1 5.5 copy-start.12
  528.6 7.8 %copy-start.5 = (f32[2,1]{0,1:T(1,128)}, f32[2,1]{0,1:T(1,128)S(1)}, u32[]{:S(2)}) copy-start(f32[2,1]{0,1:T(1,128)S(1)} %get-tuple-element.350) | copy-start | bytes 28 | tf_op jit(solution)/shard_map/while
  528.6 7.8 %copy-start.11 = (s32[8]{0:T(128)}, s32[8]{0:T(128)S(1)}, u32[]{:S(2)}) copy-start(s32[8]{0:T(128)S(1)} %get-tuple-element.351) | copy-start | bytes 100 | tf_op jit(solution)/shard_map/while
  537.7 3.7 copy-start.2
  537.7 3.7 copy-start.3
  561.0 5.5 copy-start.6
  561.0 5.5 copy-start.12
  566.5 7.8 %copy-start.5 = (f32[2,1]{0,1:T(1,128)}, f32[2,1]{0,1:T(1,128)S(1)}, u32[]{:S(2)}) copy-start(f32[2,1]{0,1:T(1,128)S(1)} %get-tuple-element.350) | copy-start | bytes 28 | tf_op jit(solution)/shard_map/while
  566.5 7.8 %copy-start.11 = (s32[8]{0:T(128)}, s32[8]{0:T(128)S(1)}, u32[]{:S(2)}) copy-start(s32[8]{0:T(128)S(1)} %get-tuple-element.351) | copy-start | bytes 100 | tf_op jit(solution)/shard_map/while
  598.8 5.5 copy-start.6
  598.8 5.5 copy-start.12
  604.4 7.8 %copy-start.5 = (f32[2,1]{0,1:T(1,128)}, f32[2,1]{0,1:T(1,128)S(1)}, u32[]{:S(2)}) copy-start(f32[2,1]{0,1:T(1,128)S(1)} %get-tuple-element.350) | copy-start | bytes 28 | tf_op jit(solution)/shard_map/while
  604.4 7.8 %copy-start.11 = (s32[8]{0:T(128)}, s32[8]{0:T(128)S(1)}, u32[]{:S(2)}) copy-start(s32[8]{0:T(128)S(1)} %get-tuple-element.351) | copy-start | bytes 100 | tf_op jit(solution)/shard_map/while
  613.4 3.7 copy-start.2
  636.7 5.5 copy-start.6
  636.7 5.5 copy-start.12
  642.3 7.8 %copy-start.5 = (f32[2,1]{0,1:T(1,128)}, f32[2,1]{0,1:T(1,128)S(1)}, u32[]{:S(2)}) copy-start(f32[2,1]{0,1:T(1,128)S(1)} %get-tuple-element.350) | copy-start | bytes 28 | tf_op jit(solution)/shard_map/while
  642.3 7.8 %copy-start.11 = (s32[8]{0:T(128)}, s32[8]{0:T(128)S(1)}, u32[]{:S(2)}) copy-start(s32[8]{0:T(128)S(1)} %get-tuple-element.351) | copy-start | bytes 100 | tf_op jit(solution)/shard_map/while
  674.6 5.5 copy-start.6
  674.6 5.5 copy-start.12
  (17 other events, 40.2 us)
Sparse Core Ops, SparseCore 0:
  11.7 2.2 sort.21.cloned.1.call-done
  (1 shorter events, 0.0 us)
Sparse Core Ops, SparseCore 1:
  274.1 22.7 all-reduce.2
  299.1 69.9 all-reduce.4
